TPU v7x, 128 devices: a whole 4x4x4 slice. The times are simulated.
128 devices in a mesh: energy: 32 (over x, z_lo, y), slab: 4 (over z_hi, core).
Axes of the slice: x: 4, y: 4, z: 4 (z_hi: 2, z_lo: 2; z = z_hi * 2 + z_lo), core: 2. Of those that a mesh axis runs over, the one named last changes fastest.
Arguments:
- green_diag: float32 [4, 1024, 2, 128, 128], P('slab', 'energy'), may hold values from -0.375 to 0.375
- green_lower: float32 [4, 1024, 2, 128, 128], P('slab', 'energy'), may hold values from -0.375 to 0.375
- green_upper: float32 [4, 1024, 2, 128, 128], P('slab', 'energy'), may hold values from -0.375 to 0.375
- sigma_lesser: float32 [4, 1024, 2, 128, 128], P('slab', 'energy'), may hold values from -6 to 6
- screened: float32 [4, 1024, 2, 128, 128], P('slab', None, None, 'energy'), may hold values from -6 to 6
- pattern: int32 [4, 128], P('slab'), may hold values 0 or 1
Outputs:
- green_lesser: float32 [4, 1024, 2, 128, 128], P('slab', 'energy')
All inputs are finite; a program needn't handle non-finite values. No bound on the sum of `pattern` on one device may be relied on, other than what follows from the above.
Results may differ from a plain program's by a relative error of at most 0.0001.
Values sent between devices are 32-bit elements; how exact they have to be, the bound alone decides.
A program may use at most 128 MiB of HBM per device.

v0:
```python
import functools
import math

import jax
import jax.numpy as jnp
import numpy as np
from jax import lax
from jax.experimental import pallas as pl
from jax.experimental.pallas import tpu as pltpu
from jax.sharding import PartitionSpec as P

BF = jnp.bfloat16
F32 = jnp.float32
B = 128
LIMIT = 60 << 20


def split(x):
    h=x.astype(BF); return h,(x-h.astype(F32)).astype(BF)
def rot(h):
    return jnp.concatenate([h, jnp.concatenate([-h[:,128:], h[:,:128]],1)],0)
def dot(a,b): return lax.dot_general(a,b,(((1,),(0,)),((),())),preferred_element_type=F32)
def dott(a,b): return lax.dot_general(a,b,(((1,),(1,)),((),())),preferred_element_type=F32)
def rotT(Tr,Ti):
    return jnp.concatenate([jnp.concatenate([Tr,-Ti],1),jnp.concatenate([Ti,Tr],1)],0)
def term(G,S):
    Gh,Gl=split(jnp.concatenate([G[0],G[1]],1)); Sh,Sl=split(jnp.concatenate([S[0],S[1]],1))
    tr,ti=G[0].T,G[1].T
    trh,trl=split(tr); tih,til=split(ti)
    Wh=rotT(trh,tih); Wl=rotT(trl,til)
    T2=dot(jnp.concatenate([Gh,Gl],0),rot(Sh)); T=T2[:128]+T2[128:]+dot(Gh,rot(Sl))
    Th,Tl=split(T)
    F2=dot(jnp.concatenate([Th,Tl],0),Wh)
    return F2[:128]+F2[128:]+dot(Th,Wl)

def dft_mats():
    a=np.arange(128); th=2*np.pi*((a[:,None]*a[None,:])%128)/128
    C,S=np.cos(th),np.sin(th)
    f=np.block([[C,S],[-S,C]]); b=np.block([[C,-S],[S,C]])
    out=[]
    for m in (f,b):
        h=m.astype(np.float32).astype(BF); l=(m-h.astype(np.float64)).astype(np.float32).astype(BF)
        out.append(np.concatenate([h,l],0))
    return np.stack(out)
def tw_tab():
    a=np.arange(128)[:,None]; p=np.arange(8)[None,:]
    th=2*np.pi*(a*p)/1024
    t=np.zeros((128,128),np.float32); t[:,:8]=np.cos(th); t[:,8:16]=np.sin(th)
    return t

R2=math.sqrt(0.5)
def radix8(x,sign):
    add=lambda u,v:(u[0]+v[0],u[1]+v[1]); sub=lambda u,v:(u[0]-v[0],u[1]-v[1])
    mi=(lambda u:(u[1],-u[0])) if sign<0 else (lambda u:(-u[1],u[0]))
    def r4(y):
        s0,d0=add(y[0],y[2]),sub(y[0],y[2]); s1,d1=add(y[1],y[3]),mi(sub(y[1],y[3]))
        return [add(s0,s1),add(d0,d1),sub(s0,s1),sub(d0,d1)]
    e=r4(x[0::2]); o=r4(x[1::2])
    def w1(u):
        m=mi(u); return ((u[0]+m[0])*R2,(u[1]+m[1])*R2)
    o=[o[0],w1(o[1]),mi(o[2]),w1(mi(o[3]))]
    return [add(e[k],o[k]) for k in range(4)]+[sub(e[k],o[k]) for k in range(4)]
def conv_r(ld_x,ld_s,st_o,tw,dm,yh,yl,v):
    for ch in range(8):
        x=[(ld_x(4*b+ch//2,0,(ch%2)*16),ld_x(4*b+ch//2,1,(ch%2)*16)) for b in range(8)]
        y=radix8(x,-1)
        rs=slice(ch*16,ch*16+16)
        for p in range(8):
            re,im=y[p]
            if p:
                c,s=tw[p,0,rs,:],tw[p,1,rs,:]
                re,im=re*c+im*s,im*c-re*s
            for k,val in enumerate((re,im)):
                h,l=split(val)
                yh[p,k*128+ch*16:k*128+ch*16+16,:]=h; yl[p,k*128+ch*16:k*128+ch*16+16,:]=l
    for pp in range(4):
        p0,p1=2*pp,2*pp+1
        H=jnp.concatenate([yh[p0],yh[p1]],1); L=jnp.concatenate([yl[p0],yl[p1]],1)
        D=dm[0]
        A=dot(D,H); Z=A[:256]+A[256:]+dot(D[:256],L)
        wr=jnp.concatenate([ld_s(p0,0),ld_s(p1,0)],1); wi=jnp.concatenate([ld_s(p0,1),ld_s(p1,1)],1)
        zr,zi=Z[:128],Z[128:]
        Q=jnp.concatenate([zr*wr-zi*wi,zr*wi+zi*wr],0)
        h,l=split(Q)
        D=dm[1]
        A=dot(D,h); V=A[:256]+A[256:]+dot(D[:256],l)
        v[p0]=V[:,:128]; v[p1]=V[:,128:]
    for ch in range(16):
        rs=slice(ch*8,ch*8+8); ri=slice(128+ch*8,128+ch*8+8)
        x=[]
        for p in range(8):
            re,im=v[p,rs,:],v[p,ri,:]
            if p:
                c,s=tw[p,0,rs,:],tw[p,1,rs,:]
                re,im=re*c-im*s,im*c+re*s
            x.append((re,im))
        y=radix8(x,1)
        for b in range(8):
            d=4*b+ch//4
            st_o(d,0,(ch%4)*8,y[b][1]*(-1.0/1024)); st_o(d,1,(ch%4)*8,y[b][0]*(1.0/1024))
def fill_tw(tab,tw):
    for p in range(1,8):
        tw[p,0]=jnp.broadcast_to(tab[:,p:p+1],(128,128)); tw[p,1]=jnp.broadcast_to(tab[:,8+p:9+p],(128,128))

E_BLOCK = 4


def diag_kernel(g, s, out):
    for k in range(E_BLOCK):
        f = term(g[k], s[k])
        out[k, 0] = f[:, :B]
        out[k, 1] = f[:, B:]


def side_kernel(spread, gl, gu, sb, sa, base, out):
    i = pl.program_id(0)
    for k in range(E_BLOCK):
        f = term(gl[k], sb[k]) + term(gu[k], sa[k])
        re = f[:, :B] + base[k, 0]
        im = f[:, B:] + base[k, 1]
        if spread:
            e = i * E_BLOCK + k
            out[pl.ds(e, B, stride=64), :] = re
            out[pl.ds(32 + e, B, stride=64), :] = im
        else:
            out[k, 0] = re
            out[k, 1] = im


def renew_kernel(sigma, conv, kept, out):
    i = pl.program_id(0)
    for k in range(E_BLOCK):
        e = i * E_BLOCK + k
        mask = kept[...]
        out[k, 0] = sigma[k, 0] + mask * conv[pl.ds(e, B, stride=64), :]
        out[k, 1] = sigma[k, 1] + mask * conv[pl.ds(32 + e, B, stride=64), :]


def conv_kernel(x, sc, dm, tab, o, tw, yh, yl, v):
    r = pl.program_id(0)

    @pl.when(r == 0)
    def _():
        fill_tw(tab, tw)

    def ld_x(s, c, r0):
        return x[s, 0, c, r0 : r0 + 16, :]

    def ld_s(p, c):
        return sc[pl.ds(p * 8 + c * 4 + r, 128, stride=64), :]

    def st_o(d, c, r0, val):
        o[d, 0, c, r0 : r0 + 8, :] = val

    conv_r(ld_x, ld_s, st_o, tw, dm, yh, yl, v)


def full(shape):
    return pl.BlockSpec(shape, lambda i: (0,) * len(shape))


PARAMS = pltpu.CompilerParams(vmem_limit_bytes=LIMIT)
E_SPEC = pl.BlockSpec((E_BLOCK, 2, B, B), lambda i: (i, 0, 0, 0))
FIELD = jax.ShapeDtypeStruct((32, 2, B, B), F32)
MOVED = jax.ShapeDtypeStruct((8192, B), F32)


def cost(terms):
    return pl.CostEstimate(flops=terms * 32 * 100_000_000, bytes_accessed=terms * 12_000_000, transcendentals=0)


def lesser_product(gd, gl, gu, sigma, spread):
    before = lax.ppermute(sigma, "slab", [(i, i + 1) for i in range(3)])
    after = lax.ppermute(sigma, "slab", [(i + 1, i) for i in range(3)])
    grid = (32 // E_BLOCK,)
    base = pl.pallas_call(
        diag_kernel, grid=grid, in_specs=[E_SPEC] * 2, out_specs=E_SPEC, out_shape=FIELD,
        compiler_params=PARAMS, cost_estimate=cost(1), name="diag",
    )(gd, sigma)
    return pl.pallas_call(
        functools.partial(side_kernel, spread), grid=grid, in_specs=[E_SPEC] * 5,
        out_specs=full((8192, B)) if spread else E_SPEC, out_shape=MOVED if spread else FIELD,
        compiler_params=PARAMS, cost_estimate=cost(2), name="sides",
    )(gl, gu, before, after, base)


def convolve(x, sc):
    bs = pl.BlockSpec((32, 1, 2, 32, B), lambda i: (0, i, 0, 0, 0))
    return pl.pallas_call(
        conv_kernel, grid=(4,),
        in_specs=[bs, full((8192, B)), full((2, 512, 256)), full((B, B))], out_specs=bs,
        out_shape=jax.ShapeDtypeStruct((32, 4, 2, 32, B), F32),
        scratch_shapes=[
            pltpu.VMEM((8, 2, B, B), F32), pltpu.VMEM((8, 256, B), BF),
            pltpu.VMEM((8, 256, B), BF), pltpu.VMEM((8, 256, B), F32),
        ],
        compiler_params=PARAMS, name="convolve",
    )(x, sc, jnp.asarray(dft_mats()), jnp.asarray(tw_tab()))


def local(green_diag, green_lower, green_upper, sigma_lesser, screened, pattern):
    gd, gl, gu, sigma = green_diag[0], green_lower[0], green_upper[0], sigma_lesser[0]
    first = lesser_product(gd, gl, gu, sigma, True).reshape(32, 4, 2, 32, B)
    moved = lax.all_to_all(first, "energy", split_axis=0, concat_axis=0, tiled=True)
    interaction = convolve(moved, screened.reshape(8192, B))
    returned = lax.all_to_all(interaction, "energy", split_axis=0, concat_axis=0, tiled=True)
    mask = pattern[0].astype(F32)
    kept = mask[:, None] * mask[None, :]
    sigma_new = pl.pallas_call(
        renew_kernel, grid=(32 // E_BLOCK,), in_specs=[E_SPEC, full((8192, B)), full((B, B))],
        out_specs=E_SPEC, out_shape=FIELD, compiler_params=PARAMS, name="renew",
    )(sigma, returned.reshape(8192, B), kept)
    return lesser_product(gd, gl, gu, sigma_new, False)[None]


def solution(mesh):
    return jax.shard_map(
        local,
        mesh=mesh,
        in_specs=(
            P("slab", "energy", None, None, None),
            P("slab", "energy", None, None, None),
            P("slab", "energy", None, None, None),
            P("slab", "energy", None, None, None),
            P("slab", None, None, "energy", None),
            P("slab", None),
        ),
        out_specs=P("slab", "energy", None, None, None),
        check_vma=False,
    )
```

profile of v0, /device:TPU:1, one launch (start us, length us, event | category | flops | bytes accessed | tf_op | source)
XLA Modules:
  0.0 279.2 jit_solution(32922615483336630)
XLA Ops:
  0.0 6.9 %collective-permute-start = (f32[32,2,128,128]{3,2,1,0:T(8,128)}, f32[32,2,128,128]{3,2,1,0:T(8,128)}, u32[]{:S(2)}, u32[]{:S(2)}) collective-permute-start(f32[32,2,128,128]{3,2,1,0:T(8,128)} %bitcast.10), channel_id=1, source_target_pairs={{0,1},{1,2},{2,3},{4,5},{5,6},{6,7},{8,9},{9,10},{10,11},{12,13},{... | collective-permute-start | bytes 12582920 | tf_op jit(solution)/shard_map/ppermute | solution.py:173
  6.9 1.9 collective-permute-start.1
  8.8 10.2 %diag.2.base = f32[32,2,128,128]{3,2,1,0:T(8,128)} custom-call(f32[32,2,128,128]{3,2,1,0:T(8,128)} %bitcast.14, f32[32,2,128,128]{3,2,1,0:T(8,128)} %bitcast.12), custom_call_target="tpu_custom_call" | custom-call | flops 3200000000 | bytes 12000000 | tf_op jit(solution)/shard_map/diag/pallas_call | solution.py:176
  19.0 56.1 %collective-permute-done.sb = f32[32,2,128,128]{3,2,1,0:T(8,128)} collective-permute-done((f32[32,2,128,128]{3,2,1,0:T(8,128)}, f32[32,2,128,128]{3,2,1,0:T(8,128)}, u32[]{:S(2)}, u32[]{:S(2)}) %collective-permute-start) | collective-permute-done | bytes 4194336 | tf_op jit(solution)/shard_map/ppermute | solution.py:173
  75.1 5.9 %collective-permute-done.1.sa = f32[32,2,128,128]{3,2,1,0:T(8,128)} collective-permute-done((f32[32,2,128,128]{3,2,1,0:T(8,128)}, f32[32,2,128,128]{3,2,1,0:T(8,128)}, u32[]{:S(2)}, u32[]{:S(2)}) %collective-permute-start.1) | collective-permute-done | bytes 4194336 | tf_op jit(solution)/shard_map/ppermute | solution.py:174
  81.0 17.1 %sides.2 = f32[8192,128]{1,0:T(8,128)} custom-call(f32[32,2,128,128]{3,2,1,0:T(8,128)} %bitcast.17, f32[32,2,128,128]{3,2,1,0:T(8,128)} %bitcast.19, f32[32,2,128,128]{3,2,1,0:T(8,128)} %collective-permute-done.sb, f32[32,2,128,128]{3,2,1,0:T(8,128)} %collective-permute-done.1.sa, f32[32,2,128,128]{3,2,1,0:T(8,128)} %diag.2.base), custom_call_target="tpu_custom_call" | custom-call | flops 6400000000 | bytes 24000000 | tf_op jit(solution)/shard_map/sides/pallas_call | solution.py:180
  98.1 48.9 %all_to_all.10.x = f32[32,4,2,32,128]{4,3,2,1,0:T(8,128)} all-to-all(f32[32,4,2,32,128]{4,3,2,1,0:T(8,128)} %bitcast.16), channel_id=1, replica_groups=mesh['energy'=32,'slab'=4] {'energy'}, dimensions={0} | all-to-all | bytes 8388608 | tf_op jit(solution)/shard_map/all_to_all | solution.py:204
  147.0 13.1 %convolve.1 = f32[32,4,2,32,128]{4,3,2,1,0:T(8,128)} custom-call(f32[32,4,2,32,128]{4,3,2,1,0:T(8,128)} %all_to_all.10.x, f32[8192,128]{1,0:T(8,128)} %bitcast.21, bf16[2,512,256]{2,1,0:T(8,128)(2,1)} %constant.4.clone.dm, f32[128,128]{1,0:T(8,128)} %constant.5.clone.tab), custom_call_target="tpu_custom_call" | custom-call | tf_op jit(solution)/shard_map/convolve/pallas_call | solution.py:189
  160.1 0.0 copy-start
  160.1 5.0 %all-to-all-start.1 = ((f32[32,4,2,32,128]{4,3,2,1,0:T(8,128)}), f32[32,4,2,32,128]{4,3,2,1,0:T(8,128)}, u32[]{:S(2)}, u32[]{:S(2)}) async-start(f32[32,4,2,32,128]{4,3,2,1,0:T(8,128)} %convolve.1), calls=%async_computation.1 | async-start | bytes 8388608 | tf_op jit(solution)/shard_map/all_to_all | solution.py:206
  165.1 0.0 copy-done
  165.1 0.7 broadcast_multiply_fusion.kept
  165.8 32.0 %all-to-all-done.1 = f32[32,4,2,32,128]{4,3,2,1,0:T(8,128)} async-done(((f32[32,4,2,32,128]{4,3,2,1,0:T(8,128)}), f32[32,4,2,32,128]{4,3,2,1,0:T(8,128)}, u32[]{:S(2)}, u32[]{:S(2)}) %all-to-all-start.1) | async-done | bytes 4194336 | tf_op jit(solution)/shard_map/all_to_all | solution.py:206
  197.9 9.9 %renew.1.s = f32[32,2,128,128]{3,2,1,0:T(8,128)} custom-call(f32[32,2,128,128]{3,2,1,0:T(8,128)} %bitcast.13, f32[8192,128]{1,0:T(8,128)} %bitcast.6.conv, f32[128,128]{1,0:T(8,128)} %broadcast_multiply_fusion.kept), custom_call_target="tpu_custom_call" | custom-call | tf_op jit(solution)/shard_map/renew/pallas_call | solution.py:209
  207.7 5.5 %collective-permute-start.2 = (f32[32,2,128,128]{3,2,1,0:T(8,128)}, f32[32,2,128,128]{3,2,1,0:T(8,128)}, u32[]{:S(2)}, u32[]{:S(2)}) collective-permute-start(f32[32,2,128,128]{3,2,1,0:T(8,128)} %renew.1.s), channel_id=1, source_target_pairs={{0,1},{1,2},{2,3},{4,5},{5,6},{6,7},{8,9},{9,10},{10,11},{12,13},{... | collective-permute-start | bytes 12582920 | tf_op jit(solution)/shard_map/ppermute | solution.py:173
  213.2 1.9 collective-permute-start.3
  215.1 10.2 %diag.3.base = f32[32,2,128,128]{3,2,1,0:T(8,128)} custom-call(f32[32,2,128,128]{3,2,1,0:T(8,128)} %bitcast.15, f32[32,2,128,128]{3,2,1,0:T(8,128)} %renew.1.s), custom_call_target="tpu_custom_call" | custom-call | flops 3200000000 | bytes 12000000 | tf_op jit(solution)/shard_map/diag/pallas_call | solution.py:176
  225.3 33.6 %collective-permute-done.2.sb = f32[32,2,128,128]{3,2,1,0:T(8,128)} collective-permute-done((f32[32,2,128,128]{3,2,1,0:T(8,128)}, f32[32,2,128,128]{3,2,1,0:T(8,128)}, u32[]{:S(2)}, u32[]{:S(2)}) %collective-permute-start.2) | collective-permute-done | bytes 4194336 | tf_op jit(solution)/shard_map/ppermute | solution.py:173
  258.9 5.9 %collective-permute-done.3.sa = f32[32,2,128,128]{3,2,1,0:T(8,128)} collective-permute-done((f32[32,2,128,128]{3,2,1,0:T(8,128)}, f32[32,2,128,128]{3,2,1,0:T(8,128)}, u32[]{:S(2)}, u32[]{:S(2)}) %collective-permute-start.3) | collective-permute-done | bytes 4194336 | tf_op jit(solution)/shard_map/ppermute | solution.py:174
  264.9 14.4 %sides.3 = f32[32,2,128,128]{3,2,1,0:T(8,128)} custom-call(f32[32,2,128,128]{3,2,1,0:T(8,128)} %bitcast.18, f32[32,2,128,128]{3,2,1,0:T(8,128)} %bitcast.20, f32[32,2,128,128]{3,2,1,0:T(8,128)} %collective-permute-done.2.sb, f32[32,2,128,128]{3,2,1,0:T(8,128)} %collective-permute-done.3.sa, f32[32,2,128,128]{3,2,1,0:T(8,128)} %diag.3.base), custom_call_target="tpu_custom_call" | custom-call | flops 6400000000 | bytes 24000000 | tf_op jit(solution)/shard_map/sides/pallas_call | solution.py:180
  (1 shorter events, 0.0 us)
Async XLA Ops:
  0.0 75.1 %collective-permute-start = (f32[32,2,128,128]{3,2,1,0:T(8,128)}, f32[32,2,128,128]{3,2,1,0:T(8,128)}, u32[]{:S(2)}, u32[]{:S(2)}) collective-permute-start(f32[32,2,128,128]{3,2,1,0:T(8,128)} %bitcast.10), channel_id=1, source_target_pairs={{0,1},{1,2},{2,3},{4,5},{5,6},{6,7},{8,9},{9,10},{10,11},{12,13},{... | collective-permute-start | bytes 12582920 | tf_op jit(solution)/shard_map/ppermute | solution.py:173
  6.9 74.1 %collective-permute-start.1 = (f32[32,2,128,128]{3,2,1,0:T(8,128)}, f32[32,2,128,128]{3,2,1,0:T(8,128)}, u32[]{:S(2)}, u32[]{:S(2)}) collective-permute-start(f32[32,2,128,128]{3,2,1,0:T(8,128)} %bitcast.11), channel_id=1, source_target_pairs={{1,0},{2,1},{3,2},{5,4},{6,5},{7,6},{9,8},{10,9},{11,10},{13,12},{... | collective-permute-start | bytes 12582920 | tf_op jit(solution)/shard_map/ppermute | solution.py:174
  160.1 5.0 %copy-start = (s32[1,128]{1,0:T(1,128)S(1)}, s32[1,128]{1,0:T(1,128)}, u32[]{:S(2)}) copy-start(s32[1,128]{1,0:T(1,128)} %param.13) | copy-start | bytes 1540
  160.1 37.8 %all-to-all-start.1 = ((f32[32,4,2,32,128]{4,3,2,1,0:T(8,128)}), f32[32,4,2,32,128]{4,3,2,1,0:T(8,128)}, u32[]{:S(2)}, u32[]{:S(2)}) async-start(f32[32,4,2,32,128]{4,3,2,1,0:T(8,128)} %convolve.1), calls=%async_computation.1 | async-start | bytes 8388608 | tf_op jit(solution)/shard_map/all_to_all | solution.py:206
  207.7 51.2 %collective-permute-start.2 = (f32[32,2,128,128]{3,2,1,0:T(8,128)}, f32[32,2,128,128]{3,2,1,0:T(8,128)}, u32[]{:S(2)}, u32[]{:S(2)}) collective-permute-start(f32[32,2,128,128]{3,2,1,0:T(8,128)} %renew.1.s), channel_id=1, source_target_pairs={{0,1},{1,2},{2,3},{4,5},{5,6},{6,7},{8,9},{9,10},{10,11},{12,13},{... | collective-permute-start | bytes 12582920 | tf_op jit(solution)/shard_map/ppermute | solution.py:173
  213.2 51.6 %collective-permute-start.3 = (f32[32,2,128,128]{3,2,1,0:T(8,128)}, f32[32,2,128,128]{3,2,1,0:T(8,128)}, u32[]{:S(2)}, u32[]{:S(2)}) collective-permute-start(f32[32,2,128,128]{3,2,1,0:T(8,128)} %renew.1.s), channel_id=1, source_target_pairs={{1,0},{2,1},{3,2},{5,4},{6,5},{7,6},{9,8},{10,9},{11,10},{13,12},{... | collective-permute-start | bytes 12582920 | tf_op jit(solution)/shard_map/ppermute | solution.py:174
where the time goes:
time: 280 us; the launch traced here: 279 us
  waiting for transfers between devices  134 us (48%)
  Pallas kernels  74.8 us (27%)
  blocking collectives  48.9 us (17%)
  starting transfers between devices  21.2 us (8%)
    ppermute x2, waiting for transfers between devices, lesser_product(): before = lax.ppermute(sigma, 'slab', [(i, i + 1) for i in range(3)])  89.7 us
    all_to_all x1, blocking collectives, local(): lax.all_to_all(first, 'energy', split_axis=0, concat_axis=0, tiled=True)  48.9 us
    all_to_all x1, waiting for transfers between devices, local(): lax.all_to_all(interaction, 'energy', split_axis=0, concat_axis=0, tiled=...  32 us
    pallas_call x2, Pallas kernels, lesser_product(): pl.pallas_call(functools.partial(side_kernel, spread), grid=grid, in_spec...  31.4 us
    pallas_call x2, Pallas kernels, lesser_product(): pl.pallas_call(diag_kernel, grid=grid, in_specs=[E_SPEC] * 2, out_specs=E...  20.4 us
    pallas_call x1, Pallas kernels, convolve(): pl.pallas_call(conv_kernel, grid=(4,), in_specs=[bs, full((8192, B)), ful...  13.1 us
    ppermute x2, starting transfers between devices, lesser_product(): before = lax.ppermute(sigma, 'slab', [(i, i + 1) for i in range(3)])  12.3 us
    ppermute x2, waiting for transfers between devices, lesser_product(): after = lax.ppermute(sigma, 'slab', [(i + 1, i) for i in range(3)])  11.8 us
  transfers between devices with their start and end apart: 5, of which 5 were waited for; matrix products, arithmetic and copies ran while one was open for 0% of the time, Pallas kernels for 7%

commit v1 on v0

--- a/solution.py
+++ b/solution.py
@@ -102,115 +102,292 @@
     for p in range(1,8):
         tw[p,0]=jnp.broadcast_to(tab[:,p:p+1],(128,128)); tw[p,1]=jnp.broadcast_to(tab[:,8+p:9+p],(128,128))
 
-E_BLOCK = 4
-
-
-def diag_kernel(g, s, out):
-    for k in range(E_BLOCK):
-        f = term(g[k], s[k])
-        out[k, 0] = f[:, :B]
-        out[k, 1] = f[:, B:]
-
-
-def side_kernel(spread, gl, gu, sb, sa, base, out):
-    i = pl.program_id(0)
-    for k in range(E_BLOCK):
-        f = term(gl[k], sb[k]) + term(gu[k], sa[k])
-        re = f[:, :B] + base[k, 0]
-        im = f[:, B:] + base[k, 1]
-        if spread:
-            e = i * E_BLOCK + k
-            out[pl.ds(e, B, stride=64), :] = re
-            out[pl.ds(32 + e, B, stride=64), :] = im
-        else:
-            out[k, 0] = re
-            out[k, 1] = im
-
-
-def renew_kernel(sigma, conv, kept, out):
-    i = pl.program_id(0)
-    for k in range(E_BLOCK):
-        e = i * E_BLOCK + k
-        mask = kept[...]
-        out[k, 0] = sigma[k, 0] + mask * conv[pl.ds(e, B, stride=64), :]
-        out[k, 1] = sigma[k, 1] + mask * conv[pl.ds(32 + e, B, stride=64), :]
-
-
-def conv_kernel(x, sc, dm, tab, o, tw, yh, yl, v):
-    r = pl.program_id(0)
-
-    @pl.when(r == 0)
-    def _():
-        fill_tw(tab, tw)
-
-    def ld_x(s, c, r0):
-        return x[s, 0, c, r0 : r0 + 16, :]
-
-    def ld_s(p, c):
-        return sc[pl.ds(p * 8 + c * 4 + r, 128, stride=64), :]
-
-    def st_o(d, c, r0, val):
-        o[d, 0, c, r0 : r0 + 8, :] = val
-
-    conv_r(ld_x, ld_s, st_o, tw, dm, yh, yl, v)
-
-
-def full(shape):
-    return pl.BlockSpec(shape, lambda i: (0,) * len(shape))
-
-
-PARAMS = pltpu.CompilerParams(vmem_limit_bytes=LIMIT)
-E_SPEC = pl.BlockSpec((E_BLOCK, 2, B, B), lambda i: (i, 0, 0, 0))
-FIELD = jax.ShapeDtypeStruct((32, 2, B, B), F32)
-MOVED = jax.ShapeDtypeStruct((8192, B), F32)
-
-
-def cost(terms):
-    return pl.CostEstimate(flops=terms * 32 * 100_000_000, bytes_accessed=terms * 12_000_000, transcendentals=0)
-
-
-def lesser_product(gd, gl, gu, sigma, spread):
-    before = lax.ppermute(sigma, "slab", [(i, i + 1) for i in range(3)])
-    after = lax.ppermute(sigma, "slab", [(i + 1, i) for i in range(3)])
-    grid = (32 // E_BLOCK,)
-    base = pl.pallas_call(
-        diag_kernel, grid=grid, in_specs=[E_SPEC] * 2, out_specs=E_SPEC, out_shape=FIELD,
-        compiler_params=PARAMS, cost_estimate=cost(1), name="diag",
-    )(gd, sigma)
-    return pl.pallas_call(
-        functools.partial(side_kernel, spread), grid=grid, in_specs=[E_SPEC] * 5,
-        out_specs=full((8192, B)) if spread else E_SPEC, out_shape=MOVED if spread else FIELD,
-        compiler_params=PARAMS, cost_estimate=cost(2), name="sides",
-    )(gl, gu, before, after, base)
-
-
-def convolve(x, sc):
-    bs = pl.BlockSpec((32, 1, 2, 32, B), lambda i: (0, i, 0, 0, 0))
-    return pl.pallas_call(
-        conv_kernel, grid=(4,),
-        in_specs=[bs, full((8192, B)), full((2, 512, 256)), full((B, B))], out_specs=bs,
-        out_shape=jax.ShapeDtypeStruct((32, 4, 2, 32, B), F32),
-        scratch_shapes=[
+ENERGY = 32
+ROWS = 8192
+CHUNK = 2048
+UNROLL = 4
+MESH = pl.DeviceIdType.MESH
+
+
+def kernel(
+    gd_h, gl_h, gu_h, s_h, sc_h, kept, dm, tab, out_h,
+    gd, gl, gu, sig, bef, aft, obuf, recv, ret, scr, tw, yh, yl, v,
+    load_sem, sc_sem, own_sem, out_sem, up_s, down_s, up_r, down_r,
+    a_s, a_r, b_s, b_r, up2_s, down2_s, up2_r, down2_r, credit,
+):
+    me = lax.axis_index("energy")
+    slab = lax.axis_index("slab")
+    first, last = slab == 0, slab == 3
+
+    def loads(k):
+        at = pl.ds(k * CHUNK, CHUNK)
+        return [
+            pltpu.make_async_copy(src.at[at], dst.at[at], load_sem.at[j, k])
+            for j, (src, dst) in enumerate(((s_h, sig), (gd_h, gd), (gl_h, gl), (gu_h, gu)))
+        ]
+
+    sc_copy = pltpu.make_async_copy(sc_h, scr, sc_sem.at[0])
+    for k in range(4):
+        for c in loads(k):
+            c.start()
+    sc_copy.start()
+
+    barrier = pltpu.get_barrier_semaphore()
+
+    def greet(d, carry):
+        pl.semaphore_signal(barrier, inc=1, device_id={"energy": lax.rem(me + d, ENERGY)}, device_id_type=MESH)
+        return carry
+
+    @pl.when(slab > 0)
+    def _():
+        pl.semaphore_signal(barrier, inc=1, device_id={"slab": slab - 1}, device_id_type=MESH)
+
+    @pl.when(slab < 3)
+    def _():
+        pl.semaphore_signal(barrier, inc=1, device_id={"slab": slab + 1}, device_id_type=MESH)
+
+    lax.fori_loop(1, ENERGY, greet, 0)
+
+    @pl.when(first)
+    def _():
+        bef[...] = jnp.zeros_like(bef)
+
+    @pl.when(last)
+    def _():
+        aft[...] = jnp.zeros_like(aft)
+
+    pl.semaphore_wait(barrier, ENERGY - 1 + jnp.where(slab > 0, 1, 0) + jnp.where(slab < 3, 1, 0))
+
+    def halo(src, k, dst, s_sem, r_sem, to):
+        at = pl.ds(k * CHUNK, CHUNK)
+        return pltpu.make_async_remote_copy(
+            src_ref=src.at[at], dst_ref=dst.at[at], send_sem=s_sem.at[k], recv_sem=r_sem.at[k],
+            device_id={"slab": to}, device_id_type=MESH,
+        )
+
+    def up(src, k, s_sem, r_sem):
+        return halo(src, k, bef, s_sem, r_sem, lax.rem(slab + 1, 4))
+
+    def down(src, k, s_sem, r_sem):
+        return halo(src, k, aft, s_sem, r_sem, lax.rem(slab + 3, 4))
+
+    for k in range(4):
+        @pl.when(slab < 3)
+        def _():
+            up(s_h, k, up_s, up_r).start()
+
+        @pl.when(slab > 0)
+        def _():
+            down(s_h, k, down_s, down_r).start()
+
+    def get(ref, e):
+        at = pl.multiple_of(e * 256, 256)
+        return ref[pl.ds(at, B), :], ref[pl.ds(at + B, B), :]
+
+    def product(e):
+        return term(get(gd, e), get(sig, e)) + term(get(gl, e), get(bef, e)) + term(get(gu, e), get(aft, e))
+
+    def arrived(k, u_r, d_r, u_s, d_s):
+        @pl.when(slab > 0)
+        def _():
+            up(sig, k, u_s, u_r).wait_recv()
+
+        @pl.when(slab < 3)
+        def _():
+            down(sig, k, d_s, d_r).wait_recv()
+
+    def a_copy(k, peer):
+        return pltpu.make_async_remote_copy(
+            src_ref=obuf.at[pl.ds(pl.multiple_of(k * CHUNK + peer * 64, 64), 64)],
+            dst_ref=recv.at[pl.ds(pl.multiple_of(me * 256 + k * 64, 64), 64)],
+            send_sem=a_s.at[0], recv_sem=a_r.at[0],
+            device_id={"energy": peer}, device_id_type=MESH,
+        )
+
+    def a_own(k):
+        return pltpu.make_async_copy(
+            obuf.at[pl.ds(pl.multiple_of(k * CHUNK + me * 64, 64), 64)],
+            recv.at[pl.ds(pl.multiple_of(me * 256 + k * 64, 64), 64)],
+            own_sem.at[k],
+        )
+
+    def first_chunk(k, carry):
+        for c in loads(k):
+            c.wait()
+        arrived(k, up_r, down_r, up_s, down_s)
+
+        def some(j, carry):
+            for u in range(UNROLL):
+                e8 = j * UNROLL + u
+                f = product(k * 8 + e8)
+                obuf[pl.ds(k * CHUNK + e8, B, stride=16), :] = f[:, :B]
+                obuf[pl.ds(k * CHUNK + 8 + e8, B, stride=16), :] = f[:, B:]
+            return carry
+
+        lax.fori_loop(0, 8 // UNROLL, some, 0)
+
+        def send(d, carry):
+            a_copy(k, lax.rem(me + d, ENERGY)).start()
+            return carry
+
+        lax.fori_loop(1, ENERGY, send, 0)
+        a_own(k).start()
+        return carry
+
+    lax.fori_loop(0, 4, first_chunk, 0)
+
+    @pl.when(slab > 0)
+    def _():
+        pl.semaphore_signal(credit.at[0], inc=1, device_id={"slab": slab - 1}, device_id_type=MESH)
+
+    @pl.when(slab < 3)
+    def _():
+        pl.semaphore_signal(credit.at[1], inc=1, device_id={"slab": slab + 1}, device_id_type=MESH)
+
+    fill_tw(tab, tw)
+    most = pl.ds(0, 31 * 256)
+    sc_copy.wait()
+    for k in range(4):
+        a_own(k).wait()
+    pltpu.make_async_copy(obuf.at[most], obuf.at[most], a_s.at[0]).wait()
+    pltpu.make_async_copy(recv.at[most], recv.at[most], a_r.at[0]).wait()
+
+    def b_copy(r, peer):
+        return pltpu.make_async_remote_copy(
+            src_ref=obuf.at[pl.ds(pl.multiple_of(peer * 256 + r * 64, 64), 64)],
+            dst_ref=ret.at[pl.ds(pl.multiple_of(me * 256 + r * 64, 64), 64)],
+            send_sem=b_s.at[0], recv_sem=b_r.at[0],
+            device_id={"energy": peer}, device_id_type=MESH,
+        )
+
+    def b_own(r):
+        at = pl.ds(pl.multiple_of(me * 256 + r * 64, 64), 64)
+        return pltpu.make_async_copy(obuf.at[at], ret.at[at], own_sem.at[4 + r])
+
+    def convolve_row(r, carry):
+        def ld_x(s, c, r0):
+            at = s * 256 + (r0 // 8) * 64 + c * 8
+            return jnp.concatenate([
+                recv[pl.ds(pl.multiple_of(at + r * 16, 8), 8), :],
+                recv[pl.ds(pl.multiple_of(at + 64 + r * 16, 8), 8), :],
+            ], 0)
+
+        def ld_s(p, c):
+            return scr[pl.ds(p * 8 + c * 4 + r, 128, stride=64), :]
+
+        def st_o(d, c, r0, val):
+            at = d * 256 + (r0 // 8) * 16 + c * 8
+            obuf[pl.ds(pl.multiple_of(at + r * 64, 8), 8), :] = val
+
+        conv_r(ld_x, ld_s, st_o, tw, dm, yh, yl, v)
+
+        def send(d, carry):
+            b_copy(r, lax.rem(me + d, ENERGY)).start()
+            return carry
+
+        lax.fori_loop(1, ENERGY, send, 0)
+        b_own(r).start()
+        return carry
+
+    lax.fori_loop(0, 4, convolve_row, 0)
+    for r in range(4):
+        b_own(r).wait()
+    pltpu.make_async_copy(ret.at[most], ret.at[most], b_r.at[0]).wait()
+
+    @pl.when(slab < 3)
+    def _():
+        pl.semaphore_wait(credit.at[0], 1)
+
+    @pl.when(slab > 0)
+    def _():
+        pl.semaphore_wait(credit.at[1], 1)
+
+    def renew(k, carry):
+        def one(e8, carry):
+            mask = kept[...]
+            at = pl.multiple_of((k * 8 + e8) * 256, 256)
+            for c in range(2):
+                rows = pl.ds(at + c * B, B)
+                sig[rows, :] = sig[rows, :] + mask * ret[pl.ds(k * 16 + c * 8 + e8, B, stride=64), :]
+            return carry
+
+        lax.fori_loop(0, 8, one, 0)
+
+        @pl.when(slab < 3)
+        def _():
+            up(sig, k, up2_s, up2_r).start()
+
+        @pl.when(slab > 0)
+        def _():
+            down(sig, k, down2_s, down2_r).start()
+
+        return carry
+
+    lax.fori_loop(0, 4, renew, 0)
+
+    def out_copy(k):
+        at = pl.ds(pl.multiple_of(k * CHUNK, CHUNK), CHUNK)
+        return pltpu.make_async_copy(recv.at[at], out_h.at[at], out_sem.at[k])
+
+    def second_chunk(k, carry):
+        arrived(k, up2_r, down2_r, up2_s, down2_s)
+
+        def some(j, carry):
+            for u in range(UNROLL):
+                e = k * 8 + j * UNROLL + u
+                f = product(e)
+                at = pl.multiple_of(e * 256, 256)
+                recv[pl.ds(at, B), :] = f[:, :B]
+                recv[pl.ds(at + B, B), :] = f[:, B:]
+            return carry
+
+        lax.fori_loop(0, 8 // UNROLL, some, 0)
+        out_copy(k).start()
+        return carry
+
+    lax.fori_loop(0, 4, second_chunk, 0)
+    pltpu.make_async_copy(obuf.at[most], obuf.at[most], b_s.at[0]).wait()
+    for k in range(4):
+        @pl.when(slab < 3)
+        def _():
+            up(sig, k, up_s, up_r).wait_send()
+            up(sig, k, up2_s, up2_r).wait_send()
+
+        @pl.when(slab > 0)
+        def _():
+            down(sig, k, down_s, down_r).wait_send()
+            down(sig, k, down2_s, down2_r).wait_send()
+
+        out_copy(k).wait()
+
+
+def local(green_diag, green_lower, green_upper, sigma_lesser, screened, pattern):
+    fields = [a.reshape(ROWS, B) for a in (green_diag, green_lower, green_upper, sigma_lesser, screened)]
+    mask = pattern[0].astype(F32)
+    kept = mask[:, None] * mask[None, :]
+    hbm = pl.BlockSpec(memory_space=pl.ANY)
+    whole = pl.BlockSpec(memory_space=pltpu.VMEM)
+    field = pltpu.VMEM((ROWS, B), F32)
+    dma = pltpu.SemaphoreType.DMA
+    four = dma((4,))
+    out = pl.pallas_call(
+        kernel,
+        out_shape=jax.ShapeDtypeStruct((ROWS, B), F32),
+        in_specs=[hbm] * 5 + [whole] * 3,
+        out_specs=hbm,
+        scratch_shapes=[field] * 10 + [
             pltpu.VMEM((8, 2, B, B), F32), pltpu.VMEM((8, 256, B), BF),
             pltpu.VMEM((8, 256, B), BF), pltpu.VMEM((8, 256, B), F32),
+            dma((4, 4)), dma((1,)), dma((8,)), four, four, four, four, four,
+            dma((1,)), dma((1,)), dma((1,)), dma((1,)), four, four, four, four,
+            pltpu.SemaphoreType.REGULAR((2,)),
         ],
-        compiler_params=PARAMS, name="convolve",
-    )(x, sc, jnp.asarray(dft_mats()), jnp.asarray(tw_tab()))
-
-
-def local(green_diag, green_lower, green_upper, sigma_lesser, screened, pattern):
-    gd, gl, gu, sigma = green_diag[0], green_lower[0], green_upper[0], sigma_lesser[0]
-    first = lesser_product(gd, gl, gu, sigma, True).reshape(32, 4, 2, 32, B)
-    moved = lax.all_to_all(first, "energy", split_axis=0, concat_axis=0, tiled=True)
-    interaction = convolve(moved, screened.reshape(8192, B))
-    returned = lax.all_to_all(interaction, "energy", split_axis=0, concat_axis=0, tiled=True)
-    mask = pattern[0].astype(F32)
-    kept = mask[:, None] * mask[None, :]
-    sigma_new = pl.pallas_call(
-        renew_kernel, grid=(32 // E_BLOCK,), in_specs=[E_SPEC, full((8192, B)), full((B, B))],
-        out_specs=E_SPEC, out_shape=FIELD, compiler_params=PARAMS, name="renew",
-    )(sigma, returned.reshape(8192, B), kept)
-    return lesser_product(gd, gl, gu, sigma_new, False)[None]
+        compiler_params=pltpu.CompilerParams(
+            vmem_limit_bytes=63 << 20, collective_id=0, has_side_effects=True
+        ),
+        name="gw",
+    )(*fields, kept, jnp.asarray(dft_mats()), jnp.asarray(tw_tab()))
+    return out.reshape(1, 32, 2, B, B)
 
 
 def solution(mesh):

time: 280 us -> 219 us (0.78)
  Pallas kernels: 74.8 us -> 213 us
  waiting for transfers between devices: 134 us -> 0 us
  blocking collectives: 48.9 us -> 0 us
  starting transfers between devices: 21.2 us -> 0 us
  local copies, waits for them, and re-layouts: 0.01 us -> 4.7 us
    pallas_call x6 -> x1, Pallas kernels: 74.8 us -> 213 us  [local(): pl.pallas_call(kernel, out_shape=jax.ShapeDtypeStruct((ROWS, B), F32), in...]
    ppermute x4 -> x0, waiting for transfers between devices: 102 us -> none  [the longest x2 89.7 us: lesser_product(): before = lax.ppermute(sigma, 'slab', [(i, i + 1) for i in range(3)])]
    all_to_all x1 -> x0, blocking collectives: 48.9 us -> none  [local(): lax.all_to_all(first, 'energy', split_axis=0, concat_axis=0, tiled=True)]
    all_to_all x1 -> x0, waiting for transfers between devices: 32 us -> none  [local(): lax.all_to_all(interaction, 'energy', split_axis=0, concat_axis=0, tiled=...]
    ppermute x4 -> x0, starting transfers between devices: 16.2 us -> none  [the longest x2 12.3 us: lesser_product(): before = lax.ppermute(sigma, 'slab', [(i, i + 1) for i in range(3)])]
    all_to_all x1 -> x0, starting transfers between devices: 4.99 us -> none  [local(): lax.all_to_all(interaction, 'energy', split_axis=0, concat_axis=0, tiled=...]
    unnamed x2 -> x1, local copies, waits for them, and re-layouts: 0.01 us -> 4.7 us
  transfers between devices with their start and end apart: 5 -> 0, of which waited for: 5 -> 0; matrix products, arithmetic and copies ran while one was open for 0% -> 0% of each run, Pallas kernels for 7% -> 0%
where the time goes in v1:
time: 219 us
  Pallas kernels  213 us (97%)
  local copies, waits for them, and re-layouts  4.7 us (2%)
    pallas_call x1, Pallas kernels, local(): pl.pallas_call(kernel, out_shape=jax.ShapeDtypeStruct((ROWS, B), F32), in...  213 us
    unnamed x1, local copies, waits for them, and re-layouts  4.7 us

profile of v1, /device:TPU:1, one launch (start us, length us, event | category | flops | bytes accessed | tf_op | source)
XLA Modules:
  0.0 218.9 jit_solution(7041066837586965737)
XLA Ops:
  0.0 0.7 convert_bitcast_fusion
  0.7 0.7 broadcast_multiply_fusion.kept
  1.4 212.8 %gw.1 = f32[8192,128]{1,0:T(8,128)} custom-call(f32[8192,128]{1,0:T(8,128)} %bitcast.9, f32[8192,128]{1,0:T(8,128)} %bitcast.10, f32[8192,128]{1,0:T(8,128)} %bitcast.11, f32[8192,128]{1,0:T(8,128)} %bitcast.12, f32[8192,128]{1,0:T(8,128)} %bitcast.13, f32[128,128]{1,0:T(8,128)} %broadcast_multiply_fusion.kept, bf16[2,512,256]{2,1,0:T(8,128)(2,1)} %constant.4.clone.dm, ...), custom_call_target="tpu_custom_call" | custom-call | tf_op jit(solution)/shard_map/gw/pallas_call | solution.py:373
  214.2 4.7 %copy.10 = f32[1,32,2,128,128]{4,3,2,1,0:T(8,128)} copy(f32[1,32,2,128,128]{4,3,2,1,0:T(8,128)} %bitcast.8) | data formatting | bytes 8388608

commit v2 on v1

v2 whole, which is shorter than its diff:
```python
import functools
import math

import jax
import jax.numpy as jnp
import numpy as np
from jax import lax
from jax.experimental import pallas as pl
from jax.experimental.pallas import tpu as pltpu
from jax.sharding import PartitionSpec as P

BF = jnp.bfloat16
F32 = jnp.float32
B = 128
LIMIT = 60 << 20


def split(x):
    h=x.astype(BF); return h,(x-h.astype(F32)).astype(BF)
def rot(h):
    return jnp.concatenate([h, jnp.concatenate([-h[:,128:], h[:,:128]],1)],0)
def dot(a,b): return lax.dot_general(a,b,(((1,),(0,)),((),())),preferred_element_type=F32)
def dott(a,b): return lax.dot_general(a,b,(((1,),(1,)),((),())),preferred_element_type=F32)
def rotT(Tr,Ti):
    return jnp.concatenate([jnp.concatenate([Tr,-Ti],1),jnp.concatenate([Ti,Tr],1)],0)
def term(G,S):
    Gh,Gl=split(jnp.concatenate([G[0],G[1]],1)); Sh,Sl=split(jnp.concatenate([S[0],S[1]],1))
    tr,ti=G[0].T,G[1].T
    trh,trl=split(tr); tih,til=split(ti)
    Wh=rotT(trh,tih); Wl=rotT(trl,til)
    T2=dot(jnp.concatenate([Gh,Gl],0),rot(Sh)); T=T2[:128]+T2[128:]+dot(Gh,rot(Sl))
    Th,Tl=split(T)
    F2=dot(jnp.concatenate([Th,Tl],0),Wh)
    return F2[:128]+F2[128:]+dot(Th,Wl)

def dft_mats():
    a=np.arange(128); th=2*np.pi*((a[:,None]*a[None,:])%128)/128
    C,S=np.cos(th),np.sin(th)
    f=np.block([[C,S],[-S,C]]); b=np.block([[C,-S],[S,C]])
    out=[]
    for m in (f,b):
        h=m.astype(np.float32).astype(BF); l=(m-h.astype(np.float64)).astype(np.float32).astype(BF)
        out.append(np.concatenate([h,l],0))
    return np.stack(out)
def tw_tab():
    a=np.arange(128)[:,None]; p=np.arange(8)[None,:]
    th=2*np.pi*(a*p)/1024
    t=np.zeros((128,128),np.float32); t[:,:8]=np.cos(th); t[:,8:16]=np.sin(th)
    return t

R2=math.sqrt(0.5)
def radix8(x,sign):
    add=lambda u,v:(u[0]+v[0],u[1]+v[1]); sub=lambda u,v:(u[0]-v[0],u[1]-v[1])
    mi=(lambda u:(u[1],-u[0])) if sign<0 else (lambda u:(-u[1],u[0]))
    def r4(y):
        s0,d0=add(y[0],y[2]),sub(y[0],y[2]); s1,d1=add(y[1],y[3]),mi(sub(y[1],y[3]))
        return [add(s0,s1),add(d0,d1),sub(s0,s1),sub(d0,d1)]
    e=r4(x[0::2]); o=r4(x[1::2])
    def w1(u):
        m=mi(u); return ((u[0]+m[0])*R2,(u[1]+m[1])*R2)
    o=[o[0],w1(o[1]),mi(o[2]),w1(mi(o[3]))]
    return [add(e[k],o[k]) for k in range(4)]+[sub(e[k],o[k]) for k in range(4)]
def conv_r(ld_x,ld_s,st_o,scale,tw,dm,yh,yl,v):
    for ch in range(8):
        x=[(ld_x(4*b+ch//2,0,(ch%2)*16),ld_x(4*b+ch//2,1,(ch%2)*16)) for b in range(8)]
        y=radix8(x,-1)
        rs=slice(ch*16,ch*16+16)
        for p in range(8):
            re,im=y[p]
            if p:
                c,s=tw[p,0,rs,:],tw[p,1,rs,:]
                re,im=re*c+im*s,im*c-re*s
            for k,val in enumerate((re,im)):
                h,l=split(val)
                yh[p,k*128+ch*16:k*128+ch*16+16,:]=h; yl[p,k*128+ch*16:k*128+ch*16+16,:]=l
    for pp in range(4):
        p0,p1=2*pp,2*pp+1
        H=jnp.concatenate([yh[p0],yh[p1]],1); L=jnp.concatenate([yl[p0],yl[p1]],1)
        D=dm[0]
        A=dot(D,H); Z=A[:256]+A[256:]+dot(D[:256],L)
        wr=jnp.concatenate([ld_s(p0,0),ld_s(p1,0)],1); wi=jnp.concatenate([ld_s(p0,1),ld_s(p1,1)],1)
        zr,zi=Z[:128],Z[128:]
        Q=jnp.concatenate([zr*wr-zi*wi,zr*wi+zi*wr],0)
        h,l=split(Q)
        D=dm[1]
        A=dot(D,h); V=A[:256]+A[256:]+dot(D[:256],l)
        v[p0]=V[:,:128]; v[p1]=V[:,128:]
    for ch in range(16):
        rs=slice(ch*8,ch*8+8); ri=slice(128+ch*8,128+ch*8+8)
        x=[]
        for p in range(8):
            re,im=v[p,rs,:],v[p,ri,:]
            if p:
                c,s=tw[p,0,rs,:],tw[p,1,rs,:]
                re,im=re*c-im*s,im*c+re*s
            x.append((re,im))
        y=radix8(x,1)
        for b in range(8):
            d=4*b+ch//4
            st_o(d,0,(ch%4)*8,y[b][1]*(-scale)); st_o(d,1,(ch%4)*8,y[b][0]*scale)
def fill_tw(tab,tw):
    for p in range(1,8):
        tw[p,0]=jnp.broadcast_to(tab[:,p:p+1],(128,128)); tw[p,1]=jnp.broadcast_to(tab[:,8+p:9+p],(128,128))

ENERGY = 32
ROWS = 8192
CHUNK = 2048
UNROLL = 4
MESH = pl.DeviceIdType.MESH


def kernel(
    gd_h, gl_h, gu_h, s_h, sc_h, pat, row_on, dm, tab, out_h,
    gd, gn, gx, sig, near, cross, obuf, recv, ret, rx, scr, tw, yh, yl, v,
    load_sem, sc_sem, own_sem, out_sem, n_s, n_r, x_s, x_r,
    a_s, a_r, b_s, b_r, c_s, c_r, n2_s, n2_r, credit,
):
    me = lax.axis_index("energy")
    slab = lax.axis_index("slab")
    odd = lax.rem(slab, 2)
    has_cross = jnp.logical_or(slab == 1, slab == 2)
    near_slab = slab + 1 - 2 * odd
    cross_slab = 3 - slab

    def load(k, j, src, dst):
        at = pl.ds(pl.multiple_of(k * CHUNK, CHUNK), CHUNK)
        return pltpu.make_async_copy(src.at[at], dst.at[at], load_sem.at[j, k])

    sc_copy = pltpu.make_async_copy(sc_h, scr, sc_sem.at[0])
    for k in range(4):
        load(k, 0, s_h, sig).start()
        load(k, 1, gd_h, gd).start()

        @pl.when(odd == 0)
        def _():
            load(k, 2, gu_h, gn).start()
            load(k, 3, gl_h, gx).start()

        @pl.when(odd == 1)
        def _():
            load(k, 2, gl_h, gn).start()
            load(k, 3, gu_h, gx).start()

    sc_copy.start()

    barrier = pltpu.get_barrier_semaphore()
    pl.semaphore_signal(barrier, inc=1, device_id={"slab": near_slab}, device_id_type=MESH)

    @pl.when(has_cross)
    def _():
        def greet_cross(d, carry):
            pl.semaphore_signal(
                barrier, inc=1,
                device_id={"energy": lax.rem(me + d, ENERGY), "slab": cross_slab}, device_id_type=MESH,
            )
            return carry

        lax.fori_loop(0, ENERGY, greet_cross, 0)

    def greet(d, carry):
        pl.semaphore_signal(barrier, inc=1, device_id={"energy": lax.rem(me + d, ENERGY)}, device_id_type=MESH)
        return carry

    lax.fori_loop(1, ENERGY, greet, 0)

    @pl.when(jnp.logical_not(has_cross))
    def _():
        cross[...] = jnp.zeros_like(cross)

    fill_tw(tab, tw)
    pl.semaphore_wait(barrier, ENERGY + jnp.where(has_cross, ENERGY, 0))

    def halo(src, k, dst, s_sem, r_sem, to):
        at = pl.ds(pl.multiple_of(k * CHUNK, CHUNK), CHUNK)
        return pltpu.make_async_remote_copy(
            src_ref=src.at[at], dst_ref=dst.at[at], send_sem=s_sem.at[k], recv_sem=r_sem.at[k],
            device_id={"slab": to}, device_id_type=MESH,
        )

    def to_near(k):
        return halo(s_h, k, near, n_s, n_r, near_slab)

    def to_cross(k):
        return halo(s_h, k, cross, x_s, x_r, cross_slab)

    def to_near_again(k):
        return halo(sig, k, near, n2_s, n2_r, near_slab)

    for k in range(4):
        @pl.when(has_cross)
        def _():
            to_cross(k).start()

        to_near(k).start()

    def get(ref, e):
        at = pl.multiple_of(e * 256, 256)
        return ref[pl.ds(at, B), :], ref[pl.ds(at + B, B), :]

    def own_near(e):
        return term(get(gd, e), get(sig, e)) + term(get(gn, e), get(near, e))

    def each(k, body):
        def some(j, carry):
            for u in range(UNROLL):
                body(j * UNROLL + u, k * 8 + j * UNROLL + u)
            return carry

        lax.fori_loop(0, 8 // UNROLL, some, 0)

    def a_copy(k, peer):
        return pltpu.make_async_remote_copy(
            src_ref=obuf.at[pl.ds(pl.multiple_of(k * CHUNK + peer * 64, 64), 64)],
            dst_ref=recv.at[pl.ds(pl.multiple_of(me * 256 + k * 64, 64), 64)],
            send_sem=a_s.at[0], recv_sem=a_r.at[0],
            device_id={"energy": peer}, device_id_type=MESH,
        )

    def a_own(k):
        return pltpu.make_async_copy(
            obuf.at[pl.ds(pl.multiple_of(k * CHUNK + me * 64, 64), 64)],
            recv.at[pl.ds(pl.multiple_of(me * 256 + k * 64, 64), 64)],
            own_sem.at[k],
        )

    def put(ref, e, f):
        at = pl.multiple_of(e * 256, 256)
        ref[pl.ds(at, B), :] = f[:, :B]
        ref[pl.ds(at + B, B), :] = f[:, B:]

    def first_part(k, carry):
        load(k, 0, s_h, sig).wait()
        load(k, 1, gd_h, gd).wait()
        load(k, 2, gu_h, gn).wait()
        to_near(k).wait_recv()
        each(k, lambda e8, e: put(ret, e, own_near(e)))
        return carry

    lax.fori_loop(0, 4, first_part, 0)
    pl.semaphore_signal(credit.at[0], inc=1, device_id={"slab": near_slab}, device_id_type=MESH)

    def first_cross(k, carry):
        load(k, 3, gl_h, gx).wait()

        @pl.when(has_cross)
        def _():
            to_cross(k).wait_recv()

        def add(e8, e):
            f = term(get(gx, e), get(cross, e))
            re, im = get(ret, e)
            obuf[pl.ds(k * CHUNK + e8, B, stride=16), :] = re + f[:, :B]
            obuf[pl.ds(k * CHUNK + 8 + e8, B, stride=16), :] = im + f[:, B:]

        each(k, add)

        def send(d, carry):
            a_copy(k, lax.rem(me + d, ENERGY)).start()
            return carry

        lax.fori_loop(1, ENERGY, send, 0)
        a_own(k).start()
        return carry

    lax.fori_loop(0, 4, first_cross, 0)

    most = pl.ds(0, 31 * 256)
    sc_copy.wait()
    for k in range(4):
        a_own(k).wait()
    pltpu.make_async_copy(obuf.at[most], obuf.at[most], a_s.at[0]).wait()
    pltpu.make_async_copy(recv.at[most], recv.at[most], a_r.at[0]).wait()

    def b_copy(k, peer, off, size):
        return pltpu.make_async_remote_copy(
            src_ref=obuf.at[pl.ds(pl.multiple_of(k * CHUNK + peer * 64 + off, 16), size)],
            dst_ref=ret.at[pl.ds(pl.multiple_of(k * CHUNK + me * 64 + off, 16), size)],
            send_sem=b_s.at[0], recv_sem=b_r.at[k],
            device_id={"energy": peer}, device_id_type=MESH,
        )

    def c_copy(k, peer, off, size):
        return pltpu.make_async_remote_copy(
            src_ref=obuf.at[pl.ds(pl.multiple_of(k * CHUNK + peer * 64 + off, 16), size)],
            dst_ref=rx.at[pl.ds(pl.multiple_of(k * CHUNK + me * 64 + off, 16), size)],
            send_sem=c_s.at[0], recv_sem=c_r.at[k],
            device_id={"energy": peer, "slab": cross_slab}, device_id_type=MESH,
        )

    def b_own(k):
        at = pl.ds(pl.multiple_of(k * CHUNK + me * 64, 64), 64)
        return pltpu.make_async_copy(obuf.at[at], ret.at[at], own_sem.at[4 + k])

    def scatter(k, off, size):
        @pl.when(has_cross)
        def _():
            def both(d, carry):
                peer = lax.rem(me + d, ENERGY)
                b_copy(k, peer, off, size).start()
                c_copy(k, peer, off, size).start()
                return carry

            lax.fori_loop(1, ENERGY, both, 0)
            c_copy(k, me, off, size).start()

        @pl.when(jnp.logical_not(has_cross))
        def _():
            def one(d, carry):
                b_copy(k, lax.rem(me + d, ENERGY), off, size).start()
                return carry

            lax.fori_loop(1, ENERGY, one, 0)

    columns = pat[...].astype(F32)

    def convolve_row(r, carry):
        def ld_x(s, c, r0):
            at = s * 256 + (r0 // 8) * 64 + c * 8
            return jnp.concatenate([
                recv[pl.ds(pl.multiple_of(at + r * 16, 8), 8), :],
                recv[pl.ds(pl.multiple_of(at + 64 + r * 16, 8), 8), :],
            ], 0)

        def ld_s(p, c):
            return scr[pl.ds(p * 8 + c * 4 + r, 128, stride=64), :]

        def st_o(d, c, r0, val):
            at = (r0 // 8) * CHUNK + d * 64 + c * 8
            obuf[pl.ds(pl.multiple_of(at + r * 16, 8), 8), :] = val

        scale = columns * (row_on[0, me * 4 + r].astype(F32) * (1.0 / 1024))
        conv_r(ld_x, ld_s, st_o, scale, tw, dm, yh, yl, v)
        scatter(0, r * 16, 16)
        return carry

    lax.fori_loop(0, 4, convolve_row, 0)
    for k in range(1, 4):
        scatter(k, 0, 64)
    for k in range(4):
        b_own(k).start()
    pl.semaphore_wait(credit.at[0], 1)

    def out_copy(k):
        at = pl.ds(pl.multiple_of(k * CHUNK, CHUNK), CHUNK)
        return pltpu.make_async_copy(recv.at[at], out_h.at[at], out_sem.at[k])

    def update(field, new, k):
        def one(e8, carry):
            at = pl.multiple_of((k * 8 + e8) * 256, 256)
            for c in range(2):
                rows = pl.ds(at + c * B, B)
                field[rows, :] = field[rows, :] + new[pl.ds(k * CHUNK + c * 8 + e8, B, stride=16), :]
            return carry

        lax.fori_loop(0, 8, one, 0)

    def second_chunk(k, carry):
        at = pl.multiple_of(k * CHUNK, CHUNK)
        part = pl.ds(at, 31 * 64)
        b_own(k).wait()
        pltpu.make_async_copy(ret.at[part], ret.at[part], b_r.at[k]).wait()
        update(sig, ret, k)
        to_near_again(k).start()

        @pl.when(has_cross)
        def _():
            part = pl.ds(at, CHUNK)
            pltpu.make_async_copy(rx.at[part], rx.at[part], c_r.at[k]).wait()
            update(cross, rx, k)

        def own_cross(e8, e):
            put(recv, e, term(get(gd, e), get(sig, e)) + term(get(gx, e), get(cross, e)))

        each(k, own_cross)
        to_near_again(k).wait_recv()

        def add(e8, e):
            f = term(get(gn, e), get(near, e))
            re, im = get(recv, e)
            put(recv, e, jnp.concatenate([re, im], 1) + f)

        each(k, add)
        out_copy(k).start()
        return carry

    lax.fori_loop(0, 4, second_chunk, 0)
    pltpu.make_async_copy(obuf.at[most], obuf.at[most], b_s.at[0]).wait()

    @pl.when(has_cross)
    def _():
        pltpu.make_async_copy(obuf, obuf, c_s.at[0]).wait()
        for k in range(4):
            to_cross(k).wait_send()

    for k in range(4):
        to_near(k).wait_send()
        to_near_again(k).wait_send()
        out_copy(k).wait()


def local(green_diag, green_lower, green_upper, sigma_lesser, screened, pattern):
    fields = [a.reshape(ROWS, B) for a in (green_diag, green_lower, green_upper, sigma_lesser, screened)]
    hbm = pl.BlockSpec(memory_space=pl.ANY)
    whole = pl.BlockSpec(memory_space=pltpu.VMEM)
    field = pltpu.VMEM((ROWS, B), F32)
    dma = pltpu.SemaphoreType.DMA
    one, four = dma((1,)), dma((4,))
    out = pl.pallas_call(
        kernel,
        out_shape=jax.ShapeDtypeStruct((ROWS, B), F32),
        in_specs=[hbm] * 5 + [whole, pl.BlockSpec(memory_space=pltpu.SMEM), whole, whole],
        out_specs=hbm,
        scratch_shapes=[field] * 11 + [
            pltpu.VMEM((8, 2, B, B), F32), pltpu.VMEM((8, 256, B), BF),
            pltpu.VMEM((8, 256, B), BF), pltpu.VMEM((8, 256, B), F32),
            dma((4, 4)), one, dma((8,)), four, four, four, four, four,
            one, one, one, four, one, four, four, four,
            pltpu.SemaphoreType.REGULAR((1,)),
        ],
        compiler_params=pltpu.CompilerParams(
            vmem_limit_bytes=63 << 20, collective_id=0, has_side_effects=True
        ),
        name="gw",
    )(*fields, pattern, pattern, jnp.asarray(dft_mats()), jnp.asarray(tw_tab()))
    return out.reshape(1, 32, 2, B, B)


def solution(mesh):
    return jax.shard_map(
        local,
        mesh=mesh,
        in_specs=(
            P("slab", "energy", None, None, None),
            P("slab", "energy", None, None, None),
            P("slab", "energy", None, None, None),
            P("slab", "energy", None, None, None),
            P("slab", None, None, "energy", None),
            P("slab", None),
        ),
        out_specs=P("slab", "energy", None, None, None),
        check_vma=False,
    )
```

time: 219 us -> 203 us (0.927); the launches traced: 219 us -> 199 us
  Pallas kernels: 213 us -> 194 us
    pallas_call x1, Pallas kernels: 213 us -> 194 us  [local(): pl.pallas_call(kernel, out_shape=jax.ShapeDtypeStruct((ROWS, B), F32), in...]
where the time goes in v2:
time: 203 us; the launch traced here: 199 us
  Pallas kernels  194 us (96%)
  local copies, waits for them, and re-layouts  4.7 us (2%)
    pallas_call x1, Pallas kernels, local(): pl.pallas_call(kernel, out_shape=jax.ShapeDtypeStruct((ROWS, B), F32), in...  194 us
    unnamed x1, local copies, waits for them, and re-layouts  4.7 us

profile of v2, /device:TPU:1, one launch (start us, length us, event | category | flops | bytes accessed | tf_op | source)
XLA Modules:
  0.0 199.0 jit_solution(9209041383778878213)
XLA Ops:
  0.0 194.3 %gw.1 = f32[8192,128]{1,0:T(8,128)} custom-call(f32[8192,128]{1,0:T(8,128)} %bitcast.7, f32[8192,128]{1,0:T(8,128)} %bitcast.8, f32[8192,128]{1,0:T(8,128)} %bitcast.9, f32[8192,128]{1,0:T(8,128)} %bitcast.10, f32[8192,128]{1,0:T(8,128)} %bitcast.11, s32[1,128]{1,0:T(1,128)} %row_on.1, s32[1,128]{1,0:T(1,128)} %row_on.1, ...), custom_call_target="tpu_custom_call" | custom-call | tf_op jit(solution)/shard_map/gw/pallas_call | solution.py:408
  194.3 4.7 %copy.10 = f32[1,32,2,128,128]{4,3,2,1,0:T(8,128)} copy(f32[1,32,2,128,128]{4,3,2,1,0:T(8,128)} %bitcast.6) | data formatting | bytes 8388608

commit v3 on v2

--- a/solution.py
+++ b/solution.py
@@ -110,9 +110,9 @@
 
 
 def kernel(
-    gd_h, gl_h, gu_h, s_h, sc_h, pat, row_on, dm, tab, out_h,
-    gd, gn, gx, sig, near, cross, obuf, recv, ret, rx, scr, tw, yh, yl, v,
-    load_sem, sc_sem, own_sem, out_sem, n_s, n_r, x_s, x_r,
+    gd_h, gl_h, gu_h, s_h, sc_h, pat, row_on, dm_h, tab_h, out,
+    gd, gn, gx, sig, near, cross, obuf, recv, ret, rx, scr, tw, yh, yl, v, dm, tab,
+    load_sem, sc_sem, own_sem, n_s, n_r, x_s, x_r,
     a_s, a_r, b_s, b_r, c_s, c_r, n2_s, n2_r, credit,
 ):
     me = lax.axis_index("energy")
@@ -142,6 +142,10 @@
             load(k, 3, gu_h, gx).start()
 
     sc_copy.start()
+    tab_copy = pltpu.make_async_copy(tab_h, tab, sc_sem.at[1])
+    dm_copy = pltpu.make_async_copy(dm_h, dm, sc_sem.at[2])
+    tab_copy.start()
+    dm_copy.start()
 
     barrier = pltpu.get_barrier_semaphore()
     pl.semaphore_signal(barrier, inc=1, device_id={"slab": near_slab}, device_id_type=MESH)
@@ -166,7 +170,9 @@
     @pl.when(jnp.logical_not(has_cross))
     def _():
         cross[...] = jnp.zeros_like(cross)
-
+        rx[...] = jnp.zeros_like(rx)
+
+    tab_copy.wait()
     fill_tw(tab, tw)
     pl.semaphore_wait(barrier, ENERGY + jnp.where(has_cross, ENERGY, 0))
 
@@ -266,6 +272,7 @@
 
     most = pl.ds(0, 31 * 256)
     sc_copy.wait()
+    dm_copy.wait()
     for k in range(4):
         a_own(k).wait()
     pltpu.make_async_copy(obuf.at[most], obuf.at[most], a_s.at[0]).wait()
@@ -291,25 +298,26 @@
         at = pl.ds(pl.multiple_of(k * CHUNK + me * 64, 64), 64)
         return pltpu.make_async_copy(obuf.at[at], ret.at[at], own_sem.at[4 + k])
 
-    def scatter(k, off, size):
-        @pl.when(has_cross)
-        def _():
-            def both(d, carry):
-                peer = lax.rem(me + d, ENERGY)
-                b_copy(k, peer, off, size).start()
-                c_copy(k, peer, off, size).start()
-                return carry
-
-            lax.fori_loop(1, ENERGY, both, 0)
-            c_copy(k, me, off, size).start()
-
-        @pl.when(jnp.logical_not(has_cross))
-        def _():
-            def one(d, carry):
-                b_copy(k, lax.rem(me + d, ENERGY), off, size).start()
-                return carry
-
-            lax.fori_loop(1, ENERGY, one, 0)
+    def scatter_both(k, off, size):
+        def both(d, carry):
+            peer = lax.rem(me + d, ENERGY)
+            b_copy(k, peer, off, size).start()
+            c_copy(k, peer, off, size).start()
+            return carry
+
+        lax.fori_loop(1, ENERGY, both, 0)
+        c_copy(k, me, off, size).start()
+
+    def scatter_own(k):
+        def one(d, carry):
+            b_copy(k, lax.rem(me + d, ENERGY), 0, 64).start()
+            return carry
+
+        lax.fori_loop(1, ENERGY, one, 0)
+
+    @pl.when(has_cross)
+    def _():
+        pl.semaphore_signal(credit.at[1], inc=1, device_id={"slab": near_slab}, device_id_type=MESH)
 
     columns = pat[...].astype(F32)
 
@@ -330,19 +338,29 @@
 
         scale = columns * (row_on[0, me * 4 + r].astype(F32) * (1.0 / 1024))
         conv_r(ld_x, ld_s, st_o, scale, tw, dm, yh, yl, v)
-        scatter(0, r * 16, 16)
+
+        @pl.when(has_cross)
+        def _():
+            scatter_both(0, r * 16, 16)
+
         return carry
 
     lax.fori_loop(0, 4, convolve_row, 0)
-    for k in range(1, 4):
-        scatter(k, 0, 64)
+
+    @pl.when(has_cross)
+    def _():
+        for k in range(1, 4):
+            scatter_both(k, 0, 64)
+
+    @pl.when(jnp.logical_not(has_cross))
+    def _():
+        pl.semaphore_wait(credit.at[1], 1)
+        for k in range(4):
+            scatter_own(k)
+
     for k in range(4):
         b_own(k).start()
     pl.semaphore_wait(credit.at[0], 1)
-
-    def out_copy(k):
-        at = pl.ds(pl.multiple_of(k * CHUNK, CHUNK), CHUNK)
-        return pltpu.make_async_copy(recv.at[at], out_h.at[at], out_sem.at[k])
 
     def update(field, new, k):
         def one(e8, carry):
@@ -366,10 +384,11 @@
         def _():
             part = pl.ds(at, CHUNK)
             pltpu.make_async_copy(rx.at[part], rx.at[part], c_r.at[k]).wait()
-            update(cross, rx, k)
 
         def own_cross(e8, e):
-            put(recv, e, term(get(gd, e), get(sig, e)) + term(get(gx, e), get(cross, e)))
+            re, im = get(cross, e)
+            new = [rx[pl.ds(k * CHUNK + c * 8 + e8, B, stride=16), :] for c in range(2)]
+            put(recv, e, term(get(gd, e), get(sig, e)) + term(get(gx, e), (re + new[0], im + new[1])))
 
         each(k, own_cross)
         to_near_again(k).wait_recv()
@@ -377,10 +396,9 @@
         def add(e8, e):
             f = term(get(gn, e), get(near, e))
             re, im = get(recv, e)
-            put(recv, e, jnp.concatenate([re, im], 1) + f)
+            put(out, e, jnp.concatenate([re, im], 1) + f)
 
         each(k, add)
-        out_copy(k).start()
         return carry
 
     lax.fori_loop(0, 4, second_chunk, 0)
@@ -395,7 +413,6 @@
     for k in range(4):
         to_near(k).wait_send()
         to_near_again(k).wait_send()
-        out_copy(k).wait()
 
 
 def local(green_diag, green_lower, green_upper, sigma_lesser, screened, pattern):
@@ -407,18 +424,19 @@
     one, four = dma((1,)), dma((4,))
     out = pl.pallas_call(
         kernel,
-        out_shape=jax.ShapeDtypeStruct((ROWS, B), F32),
-        in_specs=[hbm] * 5 + [whole, pl.BlockSpec(memory_space=pltpu.SMEM), whole, whole],
-        out_specs=hbm,
+        out_shape=pltpu.VMEM((ROWS, B), F32),
+        in_specs=[hbm] * 5 + [whole, pl.BlockSpec(memory_space=pltpu.SMEM), hbm, hbm],
+        out_specs=whole,
         scratch_shapes=[field] * 11 + [
             pltpu.VMEM((8, 2, B, B), F32), pltpu.VMEM((8, 256, B), BF),
             pltpu.VMEM((8, 256, B), BF), pltpu.VMEM((8, 256, B), F32),
-            dma((4, 4)), one, dma((8,)), four, four, four, four, four,
+            pltpu.VMEM((2, 512, 256), BF), pltpu.VMEM((B, B), F32),
+            dma((4, 4)), dma((3,)), dma((8,)), four, four, four, four,
             one, one, one, four, one, four, four, four,
-            pltpu.SemaphoreType.REGULAR((1,)),
+            pltpu.SemaphoreType.REGULAR((2,)),
         ],
         compiler_params=pltpu.CompilerParams(
-            vmem_limit_bytes=63 << 20, collective_id=0, has_side_effects=True
+            vmem_limit_bytes=55 << 20, collective_id=0, has_side_effects=True
         ),
         name="gw",
     )(*fields, pattern, pattern, jnp.asarray(dft_mats()), jnp.asarray(tw_tab()))

time: 203 us -> 195 us (0.961)
  Pallas kernels: 194 us -> 189 us
  local copies, waits for them, and re-layouts: 4.7 us -> 2.02 us
    pallas_call x1, Pallas kernels: 194 us -> 189 us  [local(): pl.pallas_call(kernel, out_shape=pltpu.VMEM((ROWS, B), F32), in_specs=[hb...]
    unnamed x1, local copies, waits for them, and re-layouts: 4.7 us -> 2.02 us
where the time goes in v3:
time: 195 us; the launch traced here: 191 us
  Pallas kernels  189 us (97%)
  local copies, waits for them, and re-layouts  2.02 us (1%)
    pallas_call x1, Pallas kernels, local(): pl.pallas_call(kernel, out_shape=pltpu.VMEM((ROWS, B), F32), in_specs=[hb...  189 us

profile of v3, /device:TPU:1, one launch (start us, length us, event | category | flops | bytes accessed | tf_op | source)
XLA Modules:
  0.0 190.7 jit_solution(12282811678495013808)
XLA Ops:
  0.0 188.7 %gw.1 = f32[8192,128]{1,0:T(8,128)S(1)} custom-call(f32[8192,128]{1,0:T(8,128)} %bitcast.7, f32[8192,128]{1,0:T(8,128)} %bitcast.8, f32[8192,128]{1,0:T(8,128)} %bitcast.9, f32[8192,128]{1,0:T(8,128)} %bitcast.10, f32[8192,128]{1,0:T(8,128)} %bitcast.11, s32[1,128]{1,0:T(1,128)} %row_on.1, s32[1,128]{1,0:T(1,128)} %row_on.1, ...), custom_call_target="tpu_custom_call" | custom-call | tf_op jit(solution)/shard_map/gw/pallas_call | solution.py:425
  188.7 2.0 %copy.10 = f32[1,32,2,128,128]{4,3,2,1,0:T(8,128)} copy(f32[1,32,2,128,128]{4,3,2,1,0:T(8,128)S(1)} %bitcast.6) | data formatting | bytes 8388608

commit v4 on v3

--- a/solution.py
+++ b/solution.py
@@ -105,7 +105,7 @@
 ENERGY = 32
 ROWS = 8192
 CHUNK = 2048
-UNROLL = 4
+UNROLL = 8
 MESH = pl.DeviceIdType.MESH
 
 
@@ -363,14 +363,11 @@
     pl.semaphore_wait(credit.at[0], 1)
 
     def update(field, new, k):
-        def one(e8, carry):
+        for e8 in range(8):
             at = pl.multiple_of((k * 8 + e8) * 256, 256)
             for c in range(2):
                 rows = pl.ds(at + c * B, B)
                 field[rows, :] = field[rows, :] + new[pl.ds(k * CHUNK + c * 8 + e8, B, stride=16), :]
-            return carry
-
-        lax.fori_loop(0, 8, one, 0)
 
     def second_chunk(k, carry):
         at = pl.multiple_of(k * CHUNK, CHUNK)

time: 195 us -> 193 us (0.990)
  no operation moved by 1% of the time
where the time goes in v4:
time: 193 us; the launch traced here: 190 us
  Pallas kernels  188 us (97%)
  local copies, waits for them, and re-layouts  2.02 us (1%)
    pallas_call x1, Pallas kernels, local(): pl.pallas_call(kernel, out_shape=pltpu.VMEM((ROWS, B), F32), in_specs=[hb...  188 us

profile of v4, /device:TPU:1, one launch (start us, length us, event | category | flops | bytes accessed | tf_op | source)
XLA Modules:
  0.0 189.7 jit_solution(9208746554560693308)
XLA Ops:
  0.0 187.7 %gw.1 = f32[8192,128]{1,0:T(8,128)S(1)} custom-call(f32[8192,128]{1,0:T(8,128)} %bitcast.7, f32[8192,128]{1,0:T(8,128)} %bitcast.8, f32[8192,128]{1,0:T(8,128)} %bitcast.9, f32[8192,128]{1,0:T(8,128)} %bitcast.10, f32[8192,128]{1,0:T(8,128)} %bitcast.11, s32[1,128]{1,0:T(1,128)} %row_on.1, s32[1,128]{1,0:T(1,128)} %row_on.1, ...), custom_call_target="tpu_custom_call" | custom-call | tf_op jit(solution)/shard_map/gw/pallas_call | solution.py:422
  187.7 2.0 %copy.10 = f32[1,32,2,128,128]{4,3,2,1,0:T(8,128)} copy(f32[1,32,2,128,128]{4,3,2,1,0:T(8,128)S(1)} %bitcast.6) | data formatting | bytes 8388608

commit v5 on v4

--- a/solution.py
+++ b/solution.py
@@ -302,11 +302,11 @@
         def both(d, carry):
             peer = lax.rem(me + d, ENERGY)
             b_copy(k, peer, off, size).start()
-            c_copy(k, peer, off, size).start()
+            c_copy(k, lax.rem(peer + 16, ENERGY), off, size).start()
             return carry
 
         lax.fori_loop(1, ENERGY, both, 0)
-        c_copy(k, me, off, size).start()
+        c_copy(k, lax.rem(me + 16, ENERGY), off, size).start()
 
     def scatter_own(k):
         def one(d, carry):

time: 193 us -> 192 us (level)
  no operation moved by 1% of the time
where the time goes in v5:
time: 192 us; the launch traced here: 189 us
  Pallas kernels  187 us (97%)
  local copies, waits for them, and re-layouts  2.02 us (1%)
    pallas_call x1, Pallas kernels, local(): pl.pallas_call(kernel, out_shape=pltpu.VMEM((ROWS, B), F32), in_specs=[hb...  187 us

profile of v5, /device:TPU:1, one launch (start us, length us, event | category | flops | bytes accessed | tf_op | source)
XLA Modules:
  0.0 189.0 jit_solution(12084614850030928636)
XLA Ops:
  0.0 187.0 %gw.1 = f32[8192,128]{1,0:T(8,128)S(1)} custom-call(f32[8192,128]{1,0:T(8,128)} %bitcast.7, f32[8192,128]{1,0:T(8,128)} %bitcast.8, f32[8192,128]{1,0:T(8,128)} %bitcast.9, f32[8192,128]{1,0:T(8,128)} %bitcast.10, f32[8192,128]{1,0:T(8,128)} %bitcast.11, s32[1,128]{1,0:T(1,128)} %row_on.1, s32[1,128]{1,0:T(1,128)} %row_on.1, ...), custom_call_target="tpu_custom_call" | custom-call | tf_op jit(solution)/shard_map/gw/pallas_call | solution.py:422
  187.0 2.0 %copy.10 = f32[1,32,2,128,128]{4,3,2,1,0:T(8,128)} copy(f32[1,32,2,128,128]{4,3,2,1,0:T(8,128)S(1)} %bitcast.6) | data formatting | bytes 8388608
